TPU v7x, 256 devices: a whole 4x4x8 slice. The times are simulated.
256 devices in a mesh: row: 16 (over y, x), col: 16 (over z, core).
Axes of the slice: x: 4, y: 4, z: 8, core: 2. Of those that a mesh axis runs over, the one named last changes fastest.
Arguments:
- g0_values: bfloat16 [8192, 8192], P('row', 'col'), may hold values from -6 to 6
- g0_pattern: int32 [64, 64], P('row', 'col'), may hold values 0 or 1
- sigma_values: bfloat16 [16, 96, 128, 128], P('row', 'col'), may hold values from -0.0014648438 to 0.0014648438
- sigma_pairs: int32 [16, 96, 2], P('row', 'col'), may hold values from 0 to 63, as said below
- sigma_count: int32 [16, 16], P('row', 'col'), may hold values from 1 to 6, as said below
Outputs:
- g_full: bfloat16 [8192, 8192], P('row', 'col')
Inputs may be any that keep to these rules, and one draw needn't show every extreme that they name: `sigma_pairs`: slot pairs of the device at position (g, o) name blocks with block row in g * 4 to g * 4 + 3 and block column in o * 4 to o * 4 + 3; the pairs of one device are distinct. `sigma_count`: count of live slots, which are the first ones of a device.
All inputs are finite; a program needn't handle non-finite values. No bound on the sum of `g0_pattern` on one device may be relied on, other than what follows from the above.
Results may differ from a plain program's by a relative error of at most 0.0037.
Values may be sent and summed in bfloat16 or wider, within the bound.
A program may use at most 128 MiB of HBM per device.

v0:
```python
import jax
import jax.numpy as jnp
from jax import lax
from jax.sharding import PartitionSpec as P


def per_device(g0_values, g0_pattern, sigma_values, sigma_pairs, sigma_count):
    block_rows = g0_pattern.shape[0]
    block_cols = g0_pattern.shape[1]
    width = sigma_values.shape[-1]
    slot_total = sigma_values.shape[1]
    mask = jnp.repeat(jnp.repeat(g0_pattern, width, axis=0), width, axis=1)
    g0_tile = g0_values * mask.astype(jnp.bfloat16)
    panel = lax.all_gather(g0_tile, "col", axis=1, tiled=True)
    live = jnp.arange(slot_total, dtype=jnp.int32) < sigma_count[0, 0]
    local_k = jnp.where(live, sigma_pairs[0, :, 0] % block_rows, block_rows)
    local_j = sigma_pairs[0, :, 1] % block_cols
    dense = jnp.zeros((block_rows, width, block_cols, width), jnp.bfloat16)
    dense = dense.at[local_k, :, local_j, :].add(sigma_values[0], mode="drop")
    sigma_tile = dense.reshape(block_rows * width, block_cols * width)
    columns = panel
    left_sum = jnp.dot(
        columns,
        lax.all_gather(sigma_tile, "row", axis=0, tiled=True),
        preferred_element_type=jnp.float32,
    )
    left_tile = left_sum.astype(jnp.bfloat16)
    start_value = g0_tile.astype(jnp.float32)
    left_panel = lax.all_gather(left_tile, "col", axis=1, tiled=True)
    columns = left_panel
    result = start_value + jnp.dot(
        columns,
        lax.all_gather(g0_tile, "row", axis=0, tiled=True),
        preferred_element_type=jnp.float32,
    )
    return result.astype(jnp.bfloat16)


def solution(mesh):
    placed = (
        P("row", "col"),
        P("row", "col"),
        P("row", "col", None, None),
        P("row", "col", None),
        P("row", "col"),
    )
    return jax.shard_map(
        per_device, mesh=mesh, in_specs=placed, out_specs=P("row", "col"), check_vma=False
    )
```

profile of v0, /device:TPU:1, one launch (start us, length us, event | category | flops | bytes accessed | tf_op | source)
XLA Modules:
  0.0 299.8 jit_solution(1443495275628197058)
XLA Ops:
  6.5 0.0 all-gather.5.cloned.1.call-start
  6.5 0.7 convert_element_type.20
  7.2 0.6 broadcast_in_dim.14
  7.9 1.9 bitcast_multiply_fusion
  9.8 0.0 all-gather.5.cloned.1.call-update
  9.8 0.0 all-gather.7.cloned.1.call-start
  10.5 0.8 fusion.4
  11.3 0.1 broadcast_in_dim.15
  11.4 2.0 scatter_fusion
  13.4 0.4 copy.6
  13.8 0.9 copy.11
  14.7 0.0 all-gather.7.cloned.1.call-update
  14.7 0.0 all-gather.11.cloned.1.call-start
  14.8 0.7 all-gather.11.cloned.1.call-update
  15.5 0.0 copy-start
  15.5 0.0 all-gather.9.cloned.1.call-start
  15.5 54.6 %all-gather.5.cloned.1.call-done = bf16[512,8192]{1,0:T(8,128)(2,1)} async-done(((bf16[512,512]{1,0:T(8,128)(2,1)}), bf16[512,8192]{1,0:T(8,128)(2,1)}) %all-gather.5.cloned.1.call-update) | async-done | bytes 8388624 | tf_op jit(solution)/shard_map/all_gather | solution.py:14
  70.1 76.4 %all-gather.7.cloned.1.call-done = bf16[8192,512]{1,0:T(8,128)(2,1)} async-done(((bf16[512,512]{1,0:T(8,128)(2,1)}), bf16[8192,512]{1,0:T(8,128)(2,1)}) %all-gather.7.cloned.1.call-update) | async-done | bytes 8388624 | tf_op jit(solution)/shard_map/all_gather | solution.py:24
  146.4 11.1 %convolution_convert_fusion = bf16[512,512]{1,0:T(8,128)(2,1)} fusion(bf16[512,8192]{1,0:T(8,128)(2,1)} %all-gather.5.cloned.1.call-done, bf16[8192,512]{1,0:T(8,128)(2,1)} %all-gather.7.cloned.1.call-done), kind=kOutput, calls=%fused_computation.3 | convolution fusion | flops 4295229440 | bytes 17301504 | tf_op jit(solution)/shard_map/dot_general | solution.py:22
  157.5 0.0 all-gather.9.cloned.1.call-update
  157.5 66.9 %all-gather.11.cloned.1.call-done = bf16[8192,512]{1,0:T(8,128)(2,1)} async-done(((bf16[512,512]{1,0:T(8,128)(2,1)}), bf16[8192,512]{1,0:T(8,128)(2,1)}) %all-gather.11.cloned.1.call-update) | async-done | bytes 8388624 | tf_op jit(solution)/shard_map/all_gather | solution.py:33
  224.4 57.8 %all-gather.9.cloned.1.call-done = bf16[512,8192]{1,0:T(8,128)(2,1)} async-done(((bf16[512,512]{1,0:T(8,128)(2,1)}), bf16[512,8192]{1,0:T(8,128)(2,1)}) %all-gather.9.cloned.1.call-update) | async-done | bytes 8388624 | tf_op jit(solution)/shard_map/all_gather | solution.py:29
  282.2 0.0 copy-done
  282.2 11.0 %fusion = bf16[512,512]{1,0:T(8,128)(2,1)} fusion(bf16[512,8192]{1,0:T(8,128)(2,1)} %all-gather.9.cloned.1.call-done, bf16[8192,512]{1,0:T(8,128)(2,1)} %all-gather.11.cloned.1.call-done, bf16[512,512]{1,0:T(8,128)(2,1)S(1)} %copy-done), kind=kOutput, calls=%fused_computation.2 | convolution fusion | flops 4295753728 | bytes 17825792 | tf_op jit(solution)/shard_map/dot_general | solution.py:31
  (1 shorter events, 0.0 us)
Async XLA Ops:
  6.5 63.5 %all-gather.5.cloned.1.call-start = ((), (), s32[]{:S(2)}) async-start(), calls=%async_computation | async-start | bytes 8912896 | tf_op jit(solution)/shard_map/all_gather | solution.py:14
  9.8 136.7 %all-gather.7.cloned.1.call-start = ((), (), s32[]{:S(2)}) async-start(), calls=%async_computation.1 | async-start | bytes 8912896 | tf_op jit(solution)/shard_map/all_gather | solution.py:24
  14.7 209.7 %all-gather.11.cloned.1.call-start = ((), (), s32[]{:S(2)}) async-start(), calls=%async_computation.3 | async-start | bytes 8912896 | tf_op jit(solution)/shard_map/all_gather | solution.py:33
  15.5 266.8 %copy-start = (bf16[512,512]{1,0:T(8,128)(2,1)S(1)}, bf16[512,512]{1,0:T(8,128)(2,1)}, u32[]{:S(2)}) copy-start(bf16[512,512]{1,0:T(8,128)(2,1)} %bitcast_multiply_fusion) | copy-start | bytes 1572868
  15.5 266.7 %all-gather.9.cloned.1.call-start = ((), (), s32[]{:S(2)}) async-start(), calls=%async_computation.2 | async-start | bytes 8912896 | tf_op jit(solution)/shard_map/all_gather | solution.py:29
Sparse Core Ops, SparseCore 0:
  9.9 60.1 all-gather.4
  72.5 73.8 all-gather.6
  148.9 75.4 all-gather.10
  226.1 56.0 all-gather.8
where the time goes:
time: 300 us
  waiting for transfers between devices  256 us (85%)
  matrix products  22.1 us (7%)
  between operations  13.8 us (5%)
  other arithmetic  5.36 us (2%)
    all_gather x1, waiting for transfers between devices, per_device(): lax.all_gather(sigma_tile, 'row', axis=0, tiled=True)  76.4 us
    all_gather x1, waiting for transfers between devices, per_device(): lax.all_gather(g0_tile, 'row', axis=0, tiled=True)  66.9 us
    all_gather x1, waiting for transfers between devices, per_device(): left_panel = lax.all_gather(left_tile, 'col', axis=1, tiled=True)  57.8 us
    all_gather x1, waiting for transfers between devices, per_device(): panel = lax.all_gather(g0_tile, 'col', axis=1, tiled=True)  54.6 us
    dot_general x1, matrix products, per_device(): jnp.dot(columns, lax.all_gather(sigma_tile, 'row', axis=0, tiled=True), p...  11.1 us
    dot_general x1, matrix products, per_device(): jnp.dot(columns, lax.all_gather(g0_tile, 'row', axis=0, tiled=True), pref...  11 us
  transfers between devices with their start and end apart: 4, of which 4 were waited for; matrix products, arithmetic and copies ran while one was open for 5% of the time, Pallas kernels for 0%

commit v1 on v0

--- a/solution.py
+++ b/solution.py
@@ -2,6 +2,13 @@
 import jax.numpy as jnp
 from jax import lax
 from jax.sharding import PartitionSpec as P
+
+
+def draw_ports(vec, out_dim):
+    all_rows = []
+    for _ in range(lax.axis_size("col")):
+        all_rows.append(vec)
+    return jnp.concatenate(lax.all_to_all(jnp.stack(all_rows, axis=0), "col", 0, 0), axis=out_dim)
 
 
 def per_device(g0_values, g0_pattern, sigma_values, sigma_pairs, sigma_count):
@@ -26,7 +33,7 @@
     )
     left_tile = left_sum.astype(jnp.bfloat16)
     start_value = g0_tile.astype(jnp.float32)
-    left_panel = lax.all_gather(left_tile, "col", axis=1, tiled=True)
+    left_panel = draw_ports(left_tile, 1)
     columns = left_panel
     result = start_value + jnp.dot(
         columns,

time: 300 us -> 370 us (1.23)
  waiting for transfers between devices: 256 us -> 315 us
  starting transfers between devices: 0.12 us -> 7.91 us
  local copies, waits for them, and re-layouts: 2.04 us -> 6.3 us
    all_to_all x0 -> x1, waiting for transfers between devices: none -> 128 us  [draw_ports(): lax.all_to_all(jnp.stack(all_rows, axis=0), 'col', 0, 0)]
    all_gather x1 -> x0, waiting for transfers between devices: 57.8 us -> none  [per_device(): left_panel = lax.all_gather(left_tile, 'col', axis=1, tiled=True)]
    all_gather x1, waiting for transfers between devices: 66.9 us -> 55.6 us  [per_device(): lax.all_gather(g0_tile, 'row', axis=0, tiled=True)]
    all_to_all x0 -> x1, starting transfers between devices: none -> 7.83 us  [draw_ports(): lax.all_to_all(jnp.stack(all_rows, axis=0), 'col', 0, 0)]
    another operation x0 -> x1, local copies, waits for them, and re-layouts: none -> 4.04 us  [draw_ports(): jnp.stack(all_rows, axis=0)]
where the time goes in v1:
time: 370 us
  waiting for transfers between devices  315 us (85%)
  matrix products  21.3 us (6%)
  between operations  13.8 us (4%)
  starting transfers between devices  7.91 us (2%)
  local copies, waits for them, and re-layouts  6.3 us (2%)
  other arithmetic  5.36 us (1%)
    all_to_all x1, waiting for transfers between devices, draw_ports(): lax.all_to_all(jnp.stack(all_rows, axis=0), 'col', 0, 0)  128 us
    all_gather x1, waiting for transfers between devices, per_device(): lax.all_gather(sigma_tile, 'row', axis=0, tiled=True)  76.4 us
    all_gather x1, waiting for transfers between devices, per_device(): lax.all_gather(g0_tile, 'row', axis=0, tiled=True)  55.6 us
    all_gather x1, waiting for transfers between devices, per_device(): panel = lax.all_gather(g0_tile, 'col', axis=1, tiled=True)  54.6 us
    dot_general x1, matrix products, per_device(): jnp.dot(columns, lax.all_gather(g0_tile, 'row', axis=0, tiled=True), pref...  11.1 us
    dot_general x1, matrix products, per_device(): jnp.dot(columns, lax.all_gather(sigma_tile, 'row', axis=0, tiled=True), p...  10.2 us
    all_to_all x1, starting transfers between devices, draw_ports(): lax.all_to_all(jnp.stack(all_rows, axis=0), 'col', 0, 0)  7.83 us
  transfers between devices with their start and end apart: 4, of which 4 were waited for; matrix products, arithmetic and copies ran while one was open for 5% of the time, Pallas kernels for 0%

profile of v1, /device:TPU:1, one launch (start us, length us, event | category | flops | bytes accessed | tf_op | source)
XLA Modules:
  0.0 369.9 jit_solution(11557548245371235778)
XLA Ops:
  6.5 0.0 all-gather.4.cloned.1.call-start
  6.5 0.7 convert_element_type.20
  7.2 0.6 broadcast_in_dim.14
  7.9 1.9 bitcast_multiply_fusion
  9.8 0.0 all-gather.4.cloned.1.call-update
  9.8 0.0 all-gather.6.cloned.1.call-start
  10.5 0.8 fusion.4
  11.3 0.1 broadcast_in_dim.15
  11.4 2.0 scatter_fusion
  13.4 0.4 copy.6
  13.8 0.9 copy.12
  14.7 0.0 all-gather.6.cloned.1.call-update
  14.7 0.0 all-gather.8.cloned.1.call-start
  14.8 0.7 all-gather.8.cloned.1.call-update
  15.5 54.6 %all-gather.4.cloned.1.call-done = bf16[512,8192]{1,0:T(8,128)(2,1)} async-done(((bf16[512,512]{1,0:T(8,128)(2,1)}), bf16[512,8192]{1,0:T(8,128)(2,1)}) %all-gather.4.cloned.1.call-update) | async-done | bytes 8388624 | tf_op jit(solution)/shard_map/all_gather | solution.py:21
  70.1 76.4 %all-gather.6.cloned.1.call-done = bf16[8192,512]{1,0:T(8,128)(2,1)} async-done(((bf16[512,512]{1,0:T(8,128)(2,1)}), bf16[8192,512]{1,0:T(8,128)(2,1)}) %all-gather.6.cloned.1.call-update) | async-done | bytes 8388624 | tf_op jit(solution)/shard_map/all_gather | solution.py:31
  146.4 10.2 %convolution_convert_fusion = bf16[512,512]{1,0:T(8,128)(2,1)S(1)} fusion(bf16[512,8192]{1,0:T(8,128)(2,1)} %all-gather.4.cloned.1.call-done, bf16[8192,512]{1,0:T(8,128)(2,1)} %all-gather.6.cloned.1.call-done), kind=kOutput, calls=%fused_computation.3 | convolution fusion | flops 4295229440 | bytes 17301504 | tf_op jit(solution)/shard_map/dot_general | solution.py:29
  156.7 0.2 copy.7
  156.9 4.0 %stack.2 = bf16[16,512,512]{1,2,0:T(8,128)(2,1)} broadcast(bf16[512,512]{0,1:T(8,128)(2,1)S(1)} %copy.7), dimensions={1,2} | broadcast | bytes 8912896 | tf_op jit(solution)/shard_map/stack | solution.py:11
  160.9 0.0 copy-start
  161.0 7.8 %all-to-all-start = ((bf16[16,512,512]{1,2,0:T(8,128)(2,1)}), bf16[16,512,512]{1,2,0:T(8,128)(2,1)}, u32[]{:S(2)}, u32[]{:S(2)}) async-start(bf16[16,512,512]{1,2,0:T(8,128)(2,1)} %stack.2), calls=%async_computation | async-start | bytes 16777216 | tf_op jit(solution)/shard_map/all_to_all | solution.py:11
  168.8 55.6 %all-gather.8.cloned.1.call-done = bf16[8192,512]{1,0:T(8,128)(2,1)} async-done(((bf16[512,512]{1,0:T(8,128)(2,1)}), bf16[8192,512]{1,0:T(8,128)(2,1)}) %all-gather.8.cloned.1.call-update) | async-done | bytes 8388624 | tf_op jit(solution)/shard_map/all_gather | solution.py:40
  224.4 127.9 %all-to-all-done = bf16[16,512,512]{1,2,0:T(8,128)(2,1)} async-done(((bf16[16,512,512]{1,2,0:T(8,128)(2,1)}), bf16[16,512,512]{1,2,0:T(8,128)(2,1)}, u32[]{:S(2)}, u32[]{:S(2)}) %all-to-all-start) | async-done | bytes 8388640 | tf_op jit(solution)/shard_map/all_to_all | solution.py:11
  352.3 0.0 copy-done
  352.3 11.1 %fusion = bf16[512,512]{1,0:T(8,128)(2,1)} fusion(bf16[512,8192]{0,1:T(8,128)(2,1)} %bitcast.7, bf16[8192,512]{1,0:T(8,128)(2,1)} %all-gather.8.cloned.1.call-done, bf16[512,512]{1,0:T(8,128)(2,1)S(1)} %copy-done), kind=kOutput, calls=%fused_computation.2 | convolution fusion | flops 4295753728 | bytes 17825792 | tf_op jit(solution)/shard_map/dot_general | solution.py:38
  (1 shorter events, 0.0 us)
Async XLA Ops:
  6.5 63.5 %all-gather.4.cloned.1.call-start = ((), (), s32[]{:S(2)}) async-start(), calls=%async_computation.1 | async-start | bytes 8912896 | tf_op jit(solution)/shard_map/all_gather | solution.py:21
  9.8 136.7 %all-gather.6.cloned.1.call-start = ((), (), s32[]{:S(2)}) async-start(), calls=%async_computation.2 | async-start | bytes 8912896 | tf_op jit(solution)/shard_map/all_gather | solution.py:31
  14.7 209.7 %all-gather.8.cloned.1.call-start = ((), (), s32[]{:S(2)}) async-start(), calls=%async_computation.3 | async-start | bytes 8912896 | tf_op jit(solution)/shard_map/all_gather | solution.py:40
  160.9 191.4 %copy-start = (bf16[512,512]{1,0:T(8,128)(2,1)S(1)}, bf16[512,512]{1,0:T(8,128)(2,1)}, u32[]{:S(2)}) copy-start(bf16[512,512]{1,0:T(8,128)(2,1)} %bitcast_multiply_fusion) | copy-start | bytes 1572868
  161.0 191.4 %all-to-all-start = ((bf16[16,512,512]{1,2,0:T(8,128)(2,1)}), bf16[16,512,512]{1,2,0:T(8,128)(2,1)}, u32[]{:S(2)}, u32[]{:S(2)}) async-start(bf16[16,512,512]{1,2,0:T(8,128)(2,1)} %stack.2), calls=%async_computation | async-start | bytes 16777216 | tf_op jit(solution)/shard_map/all_to_all | solution.py:11
Sparse Core Ops, SparseCore 0:
  9.9 60.1 all-gather.3
  72.5 73.8 all-gather.5
  148.9 75.4 all-gather.7
